TPU v7x, 32 devices: a whole 2x2x4 slice. The times are simulated.
32 devices in a mesh: dp: 4 (over y, core), row: 2 (over x), col: 4 (over z).
Axes of the slice: x: 2, y: 2, z: 4, core: 2. Of those that a mesh axis runs over, the one named last changes fastest.
Arguments:
- tokens: float32 [16384, 1024], P(('dp', 'row', 'col')), may hold values from -6 to 6
- segment_ids: int32 [16384], P(('dp', 'row', 'col')), may hold values from 0 to 127, never falling along the last dimension, each value on 1 to 512 neighbouring positions
- cotangent: float32 [16384, 1024], P(('dp', 'row', 'col')), may hold values from -6 to 6
- weight_query: float32 [1024, 1024], P('row', 'col'), as said below
- weight_key: float32 [1024, 1024], P('row', 'col'), may hold values from -0.1875 to 0.1875
- weight_value: float32 [1024, 1024], P('row', 'col'), may hold values from -0.1875 to 0.1875
- weight_output: float32 [1024, 1024], P('row', 'col'), may hold values from -0.75 to 0.75
- weight_inner: float32 [1024, 4096], P('row', 'col'), may hold values from -0.1875 to 0.1875
- weight_outer: float32 [4096, 1024], P('row', 'col'), may hold values from -0.09375 to 0.09375
- bias_query: float32 [1024], P(('row', 'col')), may hold values from -1.5 to 1.5
- bias_value: float32 [1024], P(('row', 'col')), may hold values from -1.5 to 1.5
- bias_output: float32 [1024], P(('row', 'col')), may hold values from -1.5 to 1.5
- bias_inner: float32 [4096], P(('row', 'col')), may hold values from -1.5 to 1.5
- bias_outer: float32 [1024], P(('row', 'col')), may hold values from -1.5 to 1.5
- gain_attn: float32 [1024], P(('row', 'col')), may hold values from 0.25 to 1.75
- shift_attn: float32 [1024], P(('row', 'col')), may hold values from -1.5 to 1.5
- gain_block: float32 [1024], P(('row', 'col')), may hold values from 0.25 to 1.75
- shift_block: float32 [1024], P(('row', 'col')), may hold values from -1.5 to 1.5
- tau_num: int32 [1], replicated, may hold values from 100 to 399
- tau_den: int32 [1], replicated, may hold values from 400 to 999
Outputs:
- output: float32 [16384, 1024], P(('dp', 'row', 'col'))
- grad_tokens: float32 [16384, 1024], P(('dp', 'row', 'col'))
- grad_weight_query: float32 [1024, 1024], P('row', 'col')
- grad_weight_key: float32 [1024, 1024], P('row', 'col')
- grad_weight_value: float32 [1024, 1024], P('row', 'col')
- grad_weight_output: float32 [1024, 1024], P('row', 'col')
- grad_weight_inner: float32 [1024, 4096], P('row', 'col')
- grad_weight_outer: float32 [4096, 1024], P('row', 'col')
- grad_bias_query: float32 [1024], P(('row', 'col'))
- grad_bias_value: float32 [1024], P(('row', 'col'))
- grad_bias_output: float32 [1024], P(('row', 'col'))
- grad_bias_inner: float32 [4096], P(('row', 'col'))
- grad_bias_outer: float32 [1024], P(('row', 'col'))
- grad_gain_attn: float32 [1024], P(('row', 'col'))
- grad_shift_attn: float32 [1024], P(('row', 'col'))
- grad_gain_block: float32 [1024], P(('row', 'col'))
- grad_shift_block: float32 [1024], P(('row', 'col'))
- head_peak: float32 [16], replicated
- clipped_query: float32 [1024, 1024], P('row', 'col')
- clipped_key: float32 [1024, 1024], P('row', 'col')
Inputs may be any that keep to these rules, and one draw needn't show every extreme that they name: `segment_ids`: along the tokens the numbers never fall; each document covers 1 to 512 consecutive tokens, one exactly 512. `weight_query`: entries within 18 / sqrt(1024) in magnitude.
All inputs are finite; a program needn't handle non-finite values.
Results may differ from a plain program's by a relative error of at most 0.019.
The roundings to bfloat16 on the way count: a program that leaves them out, or rounds other values in their place, can miss the bound.
Values may be sent and summed in bfloat16 or wider, within the bound.
A program may use at most 256 MiB of HBM per device.

v0:
```python
import jax
import jax.numpy as jnp
from jax import lax
from jax.sharding import PartitionSpec as P

H = 16
DH = 64
SEQ = 512
norm_eps = 1e-12
neg_fill = -1e30


def norm_rows(values, gain_vec, shift_vec):
    center = values - jnp.mean(values, axis=-1, keepdims=True)
    spread = jnp.mean(center * center, axis=-1, keepdims=True)
    return center * lax.rsqrt(spread + norm_eps) * gain_vec + shift_vec


def gelu_exact(values):
    return jax.nn.gelu(values, approximate=False)


def apply_weight(operand, weight):
    row_count, col_count, rows_in, cols_out = weight.shape
    token_count = operand.shape[0]
    result = jnp.einsum(
        "trk,rckn->tcn",
        operand.reshape(token_count, row_count, rows_in),
        weight,
        preferred_element_type=jnp.float32,
    )
    return result.reshape(token_count, col_count * cols_out)


def apply_back(gradient, weight):
    row_count, col_count, rows_in, cols_out = weight.shape
    token_count = gradient.shape[0]
    result = jnp.einsum(
        "tcn,rckn->trk",
        gradient.reshape(token_count, col_count, cols_out),
        weight,
        preferred_element_type=jnp.float32,
    )
    return result.reshape(token_count, row_count * rows_in)


def weight_term(operand, gradient, row_count, col_count, pieces):
    token_count, width_in = operand.shape
    width_out = gradient.shape[1]
    piece_rows = width_in // (row_count * pieces)
    left_blocks = operand.reshape(token_count, row_count, pieces, piece_rows)
    right_blocks = gradient.reshape(token_count, col_count, width_out // col_count)
    term = jnp.einsum(
        "trdk,tcn->drckn", left_blocks, right_blocks, preferred_element_type=jnp.float32
    )
    return term.reshape(pieces * row_count * col_count, piece_rows, width_out // col_count)


def vector_term(vector, group_count, pieces):
    return (
        vector.reshape(group_count, pieces, -1).transpose(1, 0, 2).reshape(pieces * group_count, -1)
    )


def column_sum(gradient_low):
    return jnp.sum(gradient_low, axis=0, dtype=jnp.float32)


def to_wire(block):
    return block.astype(jnp.bfloat16)[None]


def unpack(gathered, row_count, col_count):
    matrices = tuple(
        (
            shard_item.reshape(row_count, col_count, shard_item.shape[1], shard_item.shape[2])
            for shard_item in gathered[:6]
        )
    )
    vectors = tuple((shard_item.reshape(-1).astype(jnp.float32) for shard_item in gathered[6:]))
    return matrices + vectors


def fetch_params(wire_items):
    return (
        lax.all_gather(wire_items[0], ("row", "col"), axis=0, tiled=True),
        lax.all_gather(wire_items[1], ("row", "col"), axis=0, tiled=True),
        lax.all_gather(wire_items[2], ("row", "col"), axis=0, tiled=True),
        lax.all_gather(wire_items[3], ("row", "col"), axis=0, tiled=True),
        lax.all_gather(wire_items[4], ("row", "col"), axis=0, tiled=True),
        lax.all_gather(wire_items[5], ("row", "col"), axis=0, tiled=True),
        lax.all_gather(wire_items[6], ("row", "col"), axis=0, tiled=True),
        lax.all_gather(wire_items[7], ("row", "col"), axis=0, tiled=True),
        lax.all_gather(wire_items[8], ("row", "col"), axis=0, tiled=True),
        lax.all_gather(wire_items[9], ("row", "col"), axis=0, tiled=True),
        lax.all_gather(wire_items[10], ("row", "col"), axis=0, tiled=True),
        lax.all_gather(wire_items[11], ("row", "col"), axis=0, tiled=True),
        lax.all_gather(wire_items[12], ("row", "col"), axis=0, tiled=True),
        lax.all_gather(wire_items[13], ("row", "col"), axis=0, tiled=True),
        lax.all_gather(wire_items[14], ("row", "col"), axis=0, tiled=True),
    )


def masked_scores(query_heads, key_heads, allowed):
    scores = jnp.einsum(
        "sqhd,skhd->shqk", query_heads, key_heads, preferred_element_type=jnp.float32
    ) * DH ** (-0.5)
    return jnp.where(allowed, scores, neg_fill)


def on_device(
    tokens,
    segment_ids,
    cotangent,
    weight_query,
    weight_key,
    weight_value,
    weight_output,
    weight_inner,
    weight_outer,
    bias_query,
    bias_value,
    bias_output,
    bias_inner,
    bias_outer,
    gain_attn,
    shift_attn,
    gain_block,
    shift_block,
    tau_num,
    tau_den,
):
    row_count = lax.axis_size("row")
    col_count = lax.axis_size("col")
    group_count = row_count * col_count
    wire_items = tuple(
        (
            to_wire(block)
            for block in (
                weight_query,
                weight_key,
                weight_value,
                weight_output,
                weight_inner,
                weight_outer,
                bias_query,
                bias_value,
                bias_output,
                bias_inner,
                bias_outer,
                gain_attn,
                shift_attn,
                gain_block,
                shift_block,
            )
        )
    )
    params_full = unpack(fetch_params(wire_items), row_count, col_count)
    (
        whole_query,
        whole_key,
        whole_value,
        whole_output,
        whole_inner,
        whole_outer,
        add_query,
        add_value,
        add_output,
        add_inner,
        add_outer,
        scale_attn,
        offset_attn,
        scale_block,
        offset_block,
    ) = params_full
    token_count = tokens.shape[0]
    seq_count = token_count // SEQ
    head_shape = (seq_count, SEQ, H, DH)
    token_low = tokens.astype(jnp.bfloat16)
    query_low = (apply_weight(token_low, whole_query) + add_query).astype(jnp.bfloat16)
    key_low = apply_weight(token_low, whole_key).astype(jnp.bfloat16)
    value_low = (apply_weight(token_low, whole_value) + add_value).astype(jnp.bfloat16)
    query_heads = query_low.reshape(head_shape)
    key_heads = key_low.reshape(head_shape)
    value_heads = value_low.reshape(head_shape)
    segment_rows = segment_ids.reshape(seq_count, SEQ)
    allowed = (segment_rows[:, :, None] == segment_rows[:, None, :])[:, None, :, :]
    masked = masked_scores(query_heads, key_heads, allowed)
    local_top = jnp.max(masked, axis=(0, 2, 3))
    row_top = jnp.max(masked, axis=-1, keepdims=True)
    raised = jnp.exp(masked - row_top)
    row_total = jnp.sum(raised, axis=-1, keepdims=True)
    attend = raised / row_total
    log_total = row_top + jnp.log(row_total)
    context = jnp.einsum(
        "shqk,skhd->sqhd",
        attend.astype(jnp.bfloat16),
        value_heads,
        preferred_element_type=jnp.float32,
    )
    context_low = context.reshape(token_count, H * DH).astype(jnp.bfloat16)
    first_sum = tokens + apply_weight(context_low, whole_output) + add_output
    normed = norm_rows(first_sum, scale_attn, offset_attn)
    normed_low = normed.astype(jnp.bfloat16)
    hidden_pre = apply_weight(normed_low, whole_inner) + add_inner
    activated_low = gelu_exact(hidden_pre).astype(jnp.bfloat16)
    second_sum = normed + apply_weight(activated_low, whole_outer) + add_outer
    output = norm_rows(second_sum, scale_block, offset_block)
    head_peak = lax.pmax(local_top, ("dp", "row", "col"))
    back_query, back_key, back_value, back_output, back_inner, back_outer = params_full[:6]
    grad_second, grad_scale_block, grad_offset_block = jax.vjp(
        norm_rows, second_sum, scale_block, offset_block
    )[1](cotangent)
    outer_grad_low = grad_second.astype(jnp.bfloat16)
    act_grad = apply_back(outer_grad_low, back_outer)
    hidden_grad_low = jax.vjp(gelu_exact, hidden_pre)[1](act_grad)[0].astype(jnp.bfloat16)
    normed_grad = grad_second + apply_back(hidden_grad_low, back_inner)
    grad_first, grad_scale_attn, grad_offset_attn = jax.vjp(
        norm_rows, first_sum, scale_attn, offset_attn
    )[1](normed_grad)
    branch_grad_low = grad_first.astype(jnp.bfloat16)
    context_grad_low = apply_back(branch_grad_low, back_output).astype(jnp.bfloat16)
    masked_again = masked_scores(query_heads, key_heads, allowed)
    attend_again = jnp.exp(masked_again - log_total)
    attend_low = attend_again.astype(jnp.bfloat16)
    context_grad_heads = context_grad_low.reshape(head_shape)
    value_grad = jnp.einsum(
        "shqk,sqhd->skhd", attend_low, context_grad_heads, preferred_element_type=jnp.float32
    )
    attend_grad = jnp.einsum(
        "sqhd,skhd->shqk", context_grad_heads, value_heads, preferred_element_type=jnp.float32
    )
    score_grad = attend_again * (
        attend_grad - jnp.sum(attend_again * attend_grad, axis=-1, keepdims=True)
    )
    score_grad_low = score_grad.astype(jnp.bfloat16)
    query_grad = jnp.einsum(
        "shqk,skhd->sqhd", score_grad_low, key_heads, preferred_element_type=jnp.float32
    ) * DH ** (-0.5)
    key_grad = jnp.einsum(
        "shqk,sqhd->skhd", score_grad_low, query_heads, preferred_element_type=jnp.float32
    ) * DH ** (-0.5)
    query_grad_low = query_grad.reshape(token_count, H * DH).astype(jnp.bfloat16)
    key_grad_low = key_grad.reshape(token_count, H * DH).astype(jnp.bfloat16)
    value_grad_low = value_grad.reshape(token_count, H * DH).astype(jnp.bfloat16)
    grad_tokens = (
        grad_first
        + apply_back(query_grad_low, back_query)
        + apply_back(key_grad_low, back_key)
        + apply_back(value_grad_low, back_value)
    )
    pieces = 1
    terms = (
        weight_term(token_low, query_grad_low, row_count, col_count, pieces),
        weight_term(token_low, key_grad_low, row_count, col_count, pieces),
        weight_term(token_low, value_grad_low, row_count, col_count, pieces),
        weight_term(context_low, branch_grad_low, row_count, col_count, pieces),
        weight_term(normed_low, hidden_grad_low, row_count, col_count, pieces),
        weight_term(activated_low, outer_grad_low, row_count, col_count, pieces),
        vector_term(column_sum(query_grad_low), group_count, pieces),
        vector_term(column_sum(value_grad_low), group_count, pieces),
        vector_term(column_sum(branch_grad_low), group_count, pieces),
        vector_term(column_sum(hidden_grad_low), group_count, pieces),
        vector_term(column_sum(outer_grad_low), group_count, pieces),
        vector_term(grad_scale_attn, group_count, pieces),
        vector_term(grad_offset_attn, group_count, pieces),
        vector_term(grad_scale_block, group_count, pieces),
        vector_term(grad_offset_block, group_count, pieces),
    )
    parted = (
        lax.psum_scatter(
            terms[0].astype(jnp.bfloat16), ("row", "col"), scatter_dimension=0, tiled=True
        ).astype(jnp.float32),
        lax.psum_scatter(
            terms[1].astype(jnp.bfloat16), ("row", "col"), scatter_dimension=0, tiled=True
        ).astype(jnp.float32),
        lax.psum_scatter(
            terms[2].astype(jnp.bfloat16), ("row", "col"), scatter_dimension=0, tiled=True
        ).astype(jnp.float32),
        lax.psum_scatter(
            terms[3].astype(jnp.bfloat16), ("row", "col"), scatter_dimension=0, tiled=True
        ).astype(jnp.float32),
        lax.psum_scatter(
            terms[4].astype(jnp.bfloat16), ("row", "col"), scatter_dimension=0, tiled=True
        ).astype(jnp.float32),
        lax.psum_scatter(
            terms[5].astype(jnp.bfloat16), ("row", "col"), scatter_dimension=0, tiled=True
        ).astype(jnp.float32),
        lax.psum_scatter(
            terms[6].astype(jnp.bfloat16), ("row", "col"), scatter_dimension=0, tiled=True
        ).astype(jnp.float32),
        lax.psum_scatter(
            terms[7].astype(jnp.bfloat16), ("row", "col"), scatter_dimension=0, tiled=True
        ).astype(jnp.float32),
        lax.psum_scatter(
            terms[8].astype(jnp.bfloat16), ("row", "col"), scatter_dimension=0, tiled=True
        ).astype(jnp.float32),
        lax.psum_scatter(
            terms[9].astype(jnp.bfloat16), ("row", "col"), scatter_dimension=0, tiled=True
        ).astype(jnp.float32),
        lax.psum_scatter(
            terms[10].astype(jnp.bfloat16), ("row", "col"), scatter_dimension=0, tiled=True
        ).astype(jnp.float32),
        lax.psum_scatter(
            terms[11].astype(jnp.bfloat16), ("row", "col"), scatter_dimension=0, tiled=True
        ).astype(jnp.float32),
        lax.psum_scatter(
            terms[12].astype(jnp.bfloat16), ("row", "col"), scatter_dimension=0, tiled=True
        ).astype(jnp.float32),
        lax.psum_scatter(
            terms[13].astype(jnp.bfloat16), ("row", "col"), scatter_dimension=0, tiled=True
        ).astype(jnp.float32),
        lax.psum_scatter(
            terms[14].astype(jnp.bfloat16), ("row", "col"), scatter_dimension=0, tiled=True
        ).astype(jnp.float32),
    )
    summed = (
        lax.psum(parted[0][0].astype(jnp.bfloat16), "dp").astype(jnp.float32),
        lax.psum(parted[1][0].astype(jnp.bfloat16), "dp").astype(jnp.float32),
        lax.psum(parted[2][0].astype(jnp.bfloat16), "dp").astype(jnp.float32),
        lax.psum(parted[3][0].astype(jnp.bfloat16), "dp").astype(jnp.float32),
        lax.psum(parted[4][0].astype(jnp.bfloat16), "dp").astype(jnp.float32),
        lax.psum(parted[5][0].astype(jnp.bfloat16), "dp").astype(jnp.float32),
        lax.psum(parted[6][0].astype(jnp.bfloat16), "dp").astype(jnp.float32),
        lax.psum(parted[7][0].astype(jnp.bfloat16), "dp").astype(jnp.float32),
        lax.psum(parted[8][0].astype(jnp.bfloat16), "dp").astype(jnp.float32),
        lax.psum(parted[9][0].astype(jnp.bfloat16), "dp").astype(jnp.float32),
        lax.psum(parted[10][0].astype(jnp.bfloat16), "dp").astype(jnp.float32),
        lax.psum(parted[11][0].astype(jnp.bfloat16), "dp").astype(jnp.float32),
        lax.psum(parted[12][0].astype(jnp.bfloat16), "dp").astype(jnp.float32),
        lax.psum(parted[13][0].astype(jnp.bfloat16), "dp").astype(jnp.float32),
        lax.psum(parted[14][0].astype(jnp.bfloat16), "dp").astype(jnp.float32),
    )
    tau_value = tau_num[0].astype(jnp.float32) / tau_den[0].astype(jnp.float32)
    factor = jnp.sqrt(tau_value / jnp.maximum(head_peak, tau_value))
    col_width = weight_query.shape[1]
    col_heads = (lax.axis_index("col") * col_width + jnp.arange(col_width, dtype=jnp.int32)) // DH
    column_factor = jnp.sum(
        jnp.where(
            col_heads[:, None] == jnp.arange(H, dtype=jnp.int32)[None, :], factor[None, :], 0.0
        ),
        axis=1,
    )
    return (
        output,
        grad_tokens,
        summed[0],
        summed[1],
        summed[2],
        summed[3],
        summed[4],
        summed[5],
        summed[6],
        summed[7],
        summed[8],
        summed[9],
        summed[10],
        summed[11],
        summed[12],
        summed[13],
        summed[14],
        head_peak,
        weight_query * column_factor[None, :],
        weight_key * column_factor[None, :],
    )


def solution(mesh):
    in_specs = (
        P(("dp", "row", "col"), None),
        P(("dp", "row", "col")),
        P(("dp", "row", "col"), None),
        P("row", "col"),
        P("row", "col"),
        P("row", "col"),
        P("row", "col"),
        P("row", "col"),
        P("row", "col"),
        P(("row", "col")),
        P(("row", "col")),
        P(("row", "col")),
        P(("row", "col")),
        P(("row", "col")),
        P(("row", "col")),
        P(("row", "col")),
        P(("row", "col")),
        P(("row", "col")),
        P(),
        P(),
    )
    out_specs = (
        P(("dp", "row", "col"), None),
        P(("dp", "row", "col"), None),
        P("row", "col"),
        P("row", "col"),
        P("row", "col"),
        P("row", "col"),
        P("row", "col"),
        P("row", "col"),
        P(("row", "col")),
        P(("row", "col")),
        P(("row", "col")),
        P(("row", "col")),
        P(("row", "col")),
        P(("row", "col")),
        P(("row", "col")),
        P(("row", "col")),
        P(("row", "col")),
        P(),
        P("row", "col"),
        P("row", "col"),
    )
    return jax.shard_map(
        on_device, mesh=mesh, in_specs=in_specs, out_specs=out_specs, check_vma=False
    )
```

profile of v0, /device:TPU:0, one launch (start us, length us, event | category | flops | bytes accessed | tf_op | source)
XLA Modules:
  0.0 1225.3 jit_solution(10910382905271209997)
XLA Ops:
  19.2 22.3 %all-gather.16 = bf16[8,1,128]{2,1,0:T(2,128)(2,1)S(1)} all-gather(bf16[1,1,128]{2,1,0:T(2,128)(2,1)S(1)} %convert_bitcast_fusion.16), channel_id=5, replica_groups=mesh['dp'=4,'row'=2,'col'=4] {'row','col'}, dimensions={0}, use_global_device_ids=true | all-gather | bytes 2304 | tf_op jit(solution)/shard_map/all_gather | solution.py:92
  41.5 16.7 %all-gather.15 = bf16[8,1,128]{2,1,0:T(2,128)(2,1)S(1)} all-gather(bf16[1,1,128]{2,1,0:T(2,128)(2,1)S(1)} %convert_bitcast_fusion.17), channel_id=3, replica_groups=mesh['dp'=4,'row'=2,'col'=4] {'row','col'}, dimensions={0}, use_global_device_ids=true | all-gather | bytes 2304 | tf_op jit(solution)/shard_map/all_gather | solution.py:93
  58.2 18.9 %all-gather.17 = bf16[8,1,128]{2,1,0:T(2,128)(2,1)S(1)} all-gather(bf16[1,1,128]{2,1,0:T(2,128)(2,1)S(1)} %convert_bitcast_fusion.15), channel_id=8, replica_groups=mesh['dp'=4,'row'=2,'col'=4] {'row','col'}, dimensions={0}, use_global_device_ids=true | all-gather | bytes 2304 | tf_op jit(solution)/shard_map/all_gather | solution.py:94
  77.1 16.3 %all-gather.18 = bf16[8,1,128]{2,1,0:T(2,128)(2,1)S(1)} all-gather(bf16[1,1,128]{2,1,0:T(2,128)(2,1)S(1)} %convert_bitcast_fusion.14), channel_id=9, replica_groups=mesh['dp'=4,'row'=2,'col'=4] {'row','col'}, dimensions={0}, use_global_device_ids=true | all-gather | bytes 2304 | tf_op jit(solution)/shard_map/all_gather | solution.py:97
  93.4 18.8 %all-gather.19 = bf16[8,1,128]{2,1,0:T(2,128)(2,1)S(1)} all-gather(bf16[1,1,128]{2,1,0:T(2,128)(2,1)S(1)} %convert_bitcast_fusion.13), channel_id=10, replica_groups=mesh['dp'=4,'row'=2,'col'=4] {'row','col'}, dimensions={0}, use_global_device_ids=true | all-gather | bytes 2304 | tf_op jit(solution)/shard_map/all_gather | solution.py:98
  112.3 27.1 %all-gather.20 = bf16[8,1,512]{2,1,0:T(2,128)(2,1)S(1)} all-gather(bf16[1,1,512]{2,1,0:T(2,128)(2,1)S(1)} %reshape.565), channel_id=12, replica_groups=mesh['dp'=4,'row'=2,'col'=4] {'row','col'}, dimensions={0}, use_global_device_ids=true | all-gather | bytes 9216 | tf_op jit(solution)/shard_map/all_gather | solution.py:95
  139.4 16.5 %all-gather.21 = bf16[8,1,128]{2,1,0:T(2,128)(2,1)S(1)} all-gather(bf16[1,1,128]{2,1,0:T(2,128)(2,1)S(1)} %convert_bitcast_fusion.12), channel_id=14, replica_groups=mesh['dp'=4,'row'=2,'col'=4] {'row','col'}, dimensions={0}, use_global_device_ids=true | all-gather | bytes 2304 | tf_op jit(solution)/shard_map/all_gather | solution.py:96
  156.5 18.5 %all-gather.22 = bf16[8,1,128]{2,1,0:T(2,128)(2,1)S(1)} all-gather(bf16[1,1,128]{2,1,0:T(2,128)(2,1)S(1)} %convert_bitcast_fusion.11), channel_id=15, replica_groups=mesh['dp'=4,'row'=2,'col'=4] {'row','col'}, dimensions={0}, use_global_device_ids=true | all-gather | bytes 2304 | tf_op jit(solution)/shard_map/all_gather | solution.py:99
  175.6 16.3 %all-gather.23 = bf16[8,1,128]{2,1,0:T(2,128)(2,1)S(1)} all-gather(bf16[1,1,128]{2,1,0:T(2,128)(2,1)S(1)} %convert_bitcast_fusion.10), channel_id=16, replica_groups=mesh['dp'=4,'row'=2,'col'=4] {'row','col'}, dimensions={0}, use_global_device_ids=true | all-gather | bytes 2304 | tf_op jit(solution)/shard_map/all_gather | solution.py:100
  231.1 8.4 fusion
  239.5 8.3 fusion.37
  250.0 89.6 %all-gather.41.cloned.1.call-done = bf16[16384,256]{1,0:T(8,128)(2,1)} async-done(((bf16[2048,256]{1,0:T(8,128)(2,1)}), bf16[16384,256]{1,0:T(8,128)(2,1)}) %all-gather.41.cloned.1.call-update) | async-done | bytes 8388624 | tf_op jit(solution)/shard_map/all_gather | solution.py:91
  339.6 11.7 copy.193
  358.5 106.4 %all-gather.39.cloned.1.call-done = bf16[4096,1024]{1,0:T(8,128)(2,1)} async-done(((bf16[512,1024]{1,0:T(8,128)(2,1)}), bf16[4096,1024]{1,0:T(8,128)(2,1)}) %all-gather.39.cloned.1.call-update) | async-done | bytes 8388624 | tf_op jit(solution)/shard_map/all_gather | solution.py:90
  464.9 11.4 copy.191
  483.9 25.6 %multiply_convert_fusion.1 = (bf16[512,4096]{1,0:T(8,128)(2,1)S(1)}, f32[512,4096]{1,0:T(8,128)}, f32[512,4096,1]{1,0,2:T(8,128)}) fusion(f32[4096]{0:T(1024)S(1)} %bitcast.410, bf16[4096,512,2]{1,0,2:T(8,128)(2,1)} %bitcast.352, bf16[64,2,8,512]{3,2,1,0:T(8,128)(2,1)S(1)} %bitcast.393), kind=kOutput, calls=%fused_computation.24 | convolution fusion | flops 4433379328 | bytes 30425088 | tf_op jit(solution)/shard_map/trk,rckn->tcn/dot_general | solution.py:26
  509.5 9.4 fusion.79
  525.0 14.8 %fusion.80 = (bf16[4096]{0:T(1024)(128)(2,1)}, bf16[512,4096]{1,0:T(8,128)(2,1)}) fusion(f32[512,4096]{1,0:T(8,128)} %get-tuple-element.61, bf16[4096,4,256]{2,0,1:T(8,128)(2,1)} %bitcast.350, bf16[64,4,8,256]{3,2,1,0:T(8,128)(2,1)S(1)} %bitcast.370, f32[4096]{0:T(1024)S(1)} %bitcast.411, f32[512,4096,1]{1,0,2:T(8,128)} %get-tuple-element.69), kind=kOutput, calls=%fused_computation.166 | convolution fusion | flops 4328517632 | bytes 30433280 | tf_op jit(solution)/shard_map/tcn,rckn->trk/dot_general | solution.py:38
  539.8 8.5 multiply_reduce_fusion.2
  561.8 8.9 bitcast_reduce_fusion
  575.4 9.2 fusion.71
  584.5 8.2 multiply_convert_fusion
  618.1 9.0 convert_bitcast_fusion
  627.0 11.6 copy.225
  646.8 11.7 convert_bitcast_fusion.1
  658.4 11.6 copy.222
  676.2 38.7 %pmax.7 = f32[16]{0:T(128)S(1)} all-reduce(f32[16]{0:T(128)S(1)} %copy-done.50), channel_id=1, replica_groups=mesh['dp'=4,'row'=2,'col'=4] {'dp','row','col'}, use_global_device_ids=true, to_apply=%region_51.52 | all-reduce | flops 16 | bytes 128 | tf_op jit(solution)/shard_map/pmax | solution.py:209
  715.2 37.1 %all-reduce.9 = (bf16[8,128]{1,0:T(8,128)(2,1)S(1)}, bf16[8,128]{1,0:T(8,128)(2,1)S(1)}, bf16[8,128]{1,0:T(8,128)(2,1)S(1)}, bf16[8,512]{1,0:T(8,128)(2,1)S(1)},...) all-reduce(bf16[8,128]{1,0:T(8,128)(2,1)S(1)} %convert_element_type, ...), channel_id=23, replica_groups=mesh['dp'=4,'row'=2,'col'=4] {'row','col'}, use_global_device_ids=true, to_apply=%region_24.25.clone | all-reduce | flops 12288 | bytes 49152
  768.1 70.8 %reduce-scatter.9.cloned.1.call-done = bf16[1,512,256]{2,1,0:T(8,128)(2,1)} async-done(((bf16[8,512,256]{2,1,0:T(8,128)(2,1)}), bf16[1,512,256]{2,1,0:T(8,128)(2,1)}) %reduce-scatter.9.cloned.1.call-update) | async-done | bytes 262160 | tf_op jit(solution)/shard_map/reduce_scatter | solution.py:274
  838.9 150.2 %reduce-scatter.17.cloned.1.call-done = bf16[1,2048,256]{2,1,0:T(8,128)(2,1)} async-done(((bf16[8,2048,256]{2,1,0:T(8,128)(2,1)}), bf16[1,2048,256]{2,1,0:T(8,128)(2,1)}) %reduce-scatter.17.cloned.1.call-update) | async-done | bytes 1048592 | tf_op jit(solution)/shard_map/reduce_scatter | solution.py:286
  989.1 150.1 %reduce-scatter.15.cloned.1.call-done = bf16[1,512,1024]{2,1,0:T(8,128)(2,1)} async-done(((bf16[8,512,1024]{2,1,0:T(8,128)(2,1)}), bf16[1,512,1024]{2,1,0:T(8,128)(2,1)}) %reduce-scatter.15.cloned.1.call-update) | async-done | bytes 1048592 | tf_op jit(solution)/shard_map/reduce_scatter | solution.py:283
  1149.3 60.4 %all-reduce.14.cloned.1.call-done = (bf16[512,256]{1,0:T(8,128)(2,1)}, bf16[512,256]{1,0:T(8,128)(2,1)}, bf16[512,256]{1,0:T(8,128)(2,1)}, bf16[512,256]{1,0:T(8...) async-done(((bf16[512,256]{1,0:T(8,128)(2,1)}, bf16[512,256]{1,0:T(8,128)(2,1)}, bf16[512,256]{1,0:T(8,128)(2,1)}, bf16[512,256]{1,0:T(8,128)(2,1)}, ...) | async-done | bytes 3145744 | tf_op jit(solution)/shard_map/psum | solution.py:318
  (275 shorter events, 165.9 us)
Async XLA Ops:
  7.2 185.6 %all-gather.33.cloned.1.call-start = ((), (), s32[]{:S(2)}) async-start(), calls=%async_computation.13 | async-start | bytes 2359296 | tf_op jit(solution)/shard_map/all_gather | solution.py:86
  9.2 190.2 %all-gather.35.cloned.1.call-start = ((), (), s32[]{:S(2)}) async-start(), calls=%async_computation.14 | async-start | bytes 2359296 | tf_op jit(solution)/shard_map/all_gather | solution.py:87
  11.0 198.2 %all-gather.31.cloned.1.call-start = ((), (), s32[]{:S(2)}) async-start(), calls=%async_computation.12 | async-start | bytes 2359296 | tf_op jit(solution)/shard_map/all_gather | solution.py:88
  12.9 206.2 %all-gather.37.cloned.1.call-start = ((), (), s32[]{:S(2)}) async-start(), calls=%async_computation.15 | async-start | bytes 2359296 | tf_op jit(solution)/shard_map/all_gather | solution.py:89
  14.7 324.9 %all-gather.41.cloned.1.call-start = ((), (), s32[]{:S(2)}) async-start(), calls=%async_computation.17 | async-start | bytes 9437184 | tf_op jit(solution)/shard_map/all_gather | solution.py:91
  15.9 25.6 %copy-start.52 = (f32[128]{0:T(128)S(1)}, f32[128]{0:T(128)}, u32[]{:S(2)}) copy-start(f32[128]{0:T(128)} %param.30) | copy-start | bytes 1540
  15.9 42.3 %copy-start.53 = (f32[128]{0:T(128)S(1)}, f32[128]{0:T(128)}, u32[]{:S(2)}) copy-start(f32[128]{0:T(128)} %param.31) | copy-start | bytes 1540
  15.9 61.2 %copy-start.54 = (f32[128]{0:T(128)S(1)}, f32[128]{0:T(128)}, u32[]{:S(2)}) copy-start(f32[128]{0:T(128)} %param.34) | copy-start | bytes 1540
  15.9 77.5 %copy-start.55 = (f32[128]{0:T(128)S(1)}, f32[128]{0:T(128)}, u32[]{:S(2)}) copy-start(f32[128]{0:T(128)} %param.35) | copy-start | bytes 1540
  15.9 96.4 %copy-start.49 = (f32[512]{0:T(512)S(1)}, f32[512]{0:T(512)}, u32[]{:S(2)}) copy-start(f32[512]{0:T(512)} %param.32) | copy-start | bytes 6148
  15.9 123.4 %copy-start.56 = (f32[128]{0:T(128)S(1)}, f32[128]{0:T(128)}, u32[]{:S(2)}) copy-start(f32[128]{0:T(128)} %param.33) | copy-start | bytes 1540
  15.9 140.6 %copy-start.57 = (f32[128]{0:T(128)S(1)}, f32[128]{0:T(128)}, u32[]{:S(2)}) copy-start(f32[128]{0:T(128)} %param.36) | copy-start | bytes 1540
  15.9 159.7 %copy-start.58 = (f32[128]{0:T(128)S(1)}, f32[128]{0:T(128)}, u32[]{:S(2)}) copy-start(f32[128]{0:T(128)} %param.37) | copy-start | bytes 1540
  15.9 176.6 %copy-start.41 = (s32[512]{0:T(512)S(1)}, s32[512]{0:T(512)}, u32[]{:S(2)}) copy-start(s32[512]{0:T(512)} %param.21) | copy-start | bytes 6148
  16.0 448.9 %all-gather.39.cloned.1.call-start = ((), (), s32[]{:S(2)}) async-start(), calls=%async_computation.16 | async-start | bytes 9437184 | tf_op jit(solution)/shard_map/all_gather | solution.py:90
  18.9 747.4 %reduce-scatter.13.cloned.1.call-start = ((), (), s32[]{:S(2)}) async-start(), calls=%async_computation.9 | async-start | bytes 2359296 | tf_op jit(solution)/shard_map/reduce_scatter | solution.py:280
  19.1 194.6 %copy-start.23 = (bf16[512,1024]{1,0:T(8,128)(2,1)}, bf16[512,1024]{1,0:T(8,128)(2,1)S(1)}, u32[]{:S(2)}) copy-start(bf16[512,1024]{1,0:T(8,128)(2,1)S(1)} %convert_element_type.490) | copy-start | bytes 3145732
  250.0 233.8 %copy-start.28 = (bf16[512,1024]{1,0:T(8,128)(2,1)}, bf16[512,1024]{1,0:T(8,128)(2,1)S(1)}, u32[]{:S(2)}) copy-start(bf16[512,1024]{1,0:T(8,128)(2,1)S(1)} %fusion.32) | copy-start | bytes 3145732
  483.9 25.6 %copy-start.46 = (f32[8,1,128]{2,1,0:T(1,128)S(1)}, f32[8,1,128]{2,1,0:T(1,128)}, u32[]{:S(2)}) copy-start(f32[8,1,128]{2,1,0:T(1,128)} %convert_element_type.645) | copy-start | bytes 12292
  559.1 207.2 %reduce-scatter.11.cloned.1.call-start = ((), (), s32[]{:S(2)}) async-start(), calls=%async_computation.8 | async-start | bytes 2359296 | tf_op jit(solution)/shard_map/reduce_scatter | solution.py:277
  575.3 192.7 %reduce-scatter.7.cloned.1.call-start = ((), (), s32[]{:S(2)}) async-start(), calls=%async_computation.6 | async-start | bytes 2359296 | tf_op jit(solution)/shard_map/reduce_scatter | solution.py:271
  602.9 236.0 %reduce-scatter.9.cloned.1.call-start = ((), (), s32[]{:S(2)}) async-start(), calls=%async_computation.7 | async-start | bytes 2359296 | tf_op jit(solution)/shard_map/reduce_scatter | solution.py:274
  617.2 371.9 %reduce-scatter.17.cloned.1.call-start = ((), (), s32[]{:S(2)}) async-start(), calls=%async_computation.11 | async-start | bytes 9437184 | tf_op jit(solution)/shard_map/reduce_scatter | solution.py:286
  638.7 500.5 %reduce-scatter.15.cloned.1.call-start = ((), (), s32[]{:S(2)}) async-start(), calls=%async_computation.10 | async-start | bytes 9437184 | tf_op jit(solution)/shard_map/reduce_scatter | solution.py:283
  670.1 539.6 %all-reduce.14.cloned.1.call-start = ((), (), s32[]{:S(2)}) async-start(), calls=%async_computation.18 | async-start | bytes 6291456 | tf_op jit(solution)/shard_map/psum | solution.py:318
  674.6 40.5 %copy-start.45 = (bf16[4096]{0:T(1024)(128)(2,1)S(1)}, bf16[4096]{0:T(1024)(128)(2,1)}, u32[]{:S(2)}) copy-start(bf16[4096]{0:T(1024)(128)(2,1)} %get-tuple-element.78) | copy-start | bytes 24580
  674.6 40.6 %copy-start.42 = (bf16[1024]{0:T(1024)(128)(2,1)S(1)}, bf16[1024]{0:T(1024)(128)(2,1)}, u32[]{:S(2)}) copy-start(bf16[1024]{0:T(1024)(128)(2,1)} %get-tuple-element.26) | copy-start | bytes 6148
  674.6 40.6 %copy-start.43 = (bf16[1024]{0:T(1024)(128)(2,1)S(1)}, bf16[1024]{0:T(1024)(128)(2,1)}, u32[]{:S(2)}) copy-start(bf16[1024]{0:T(1024)(128)(2,1)} %get-tuple-element.52) | copy-start | bytes 6148
  674.6 40.6 %copy-start.44 = (bf16[1024]{0:T(1024)(128)(2,1)S(1)}, bf16[1024]{0:T(1024)(128)(2,1)}, u32[]{:S(2)}) copy-start(bf16[1024]{0:T(1024)(128)(2,1)} %get-tuple-element.54) | copy-start | bytes 6148
  674.6 40.6 %copy-start.47 = (bf16[1024]{0:T(1024)(128)(2,1)S(1)}, bf16[1024]{0:T(1024)(128)(2,1)}, u32[]{:S(2)}) copy-start(bf16[1024]{0:T(1024)(128)(2,1)} %get-tuple-element.24) | copy-start | bytes 6148
  674.6 40.6 %copy-start.48 = (bf16[1024]{0:T(1024)(128)(2,1)S(1)}, bf16[1024]{0:T(1024)(128)(2,1)}, u32[]{:S(2)}) copy-start(bf16[1024]{0:T(1024)(128)(2,1)} %get-tuple-element.27) | copy-start | bytes 6148
  714.9 429.6 %copy-start.63 = (f32[16]{0:T(128)}, f32[16]{0:T(128)S(1)}, u32[]{:S(2)}) copy-start(f32[16]{0:T(128)S(1)} %pmax.7) | copy-start | bytes 196
  (47 other events, 293.1 us)
Sparse Core Ops, SparseCore 0:
  10.7 51.8 all-gather.32
  65.3 47.7 all-gather.34
  115.8 47.7 all-gather.30
  166.1 47.9 all-gather.36
  216.6 122.9 all-gather.40
  342.2 122.6 all-gather.38
  559.3 66.4 reduce-scatter.12
  629.3 67.8 reduce-scatter.10
  700.7 67.3 reduce-scatter.6
  771.4 67.4 reduce-scatter.8
  842.5 146.5 reduce-scatter.16
  992.6 146.5 reduce-scatter.14
  1142.0 67.6 all-reduce.13
where the time goes:
time: 1240 us; the launch traced here: 1230 us
  waiting for transfers between devices  630 us (51%)
  blocking collectives  253 us (20%)
  matrix products  149 us (12%)
  local copies, waits for them, and re-layouts  123 us (10%)
  other arithmetic  52.9 us (4%)
  between operations  16.5 us (1%)
    reduce_scatter x1, waiting for transfers between devices, on_device(): lax.psum_scatter(terms[5].astype(jnp.bfloat16), ('row', 'col'), scatter_d...  150 us
    reduce_scatter x1, waiting for transfers between devices, on_device(): lax.psum_scatter(terms[4].astype(jnp.bfloat16), ('row', 'col'), scatter_d...  150 us
    all_gather x1, waiting for transfers between devices, fetch_params(): lax.all_gather(wire_items[4], ('row', 'col'), axis=0, tiled=True)  106 us
    all_gather x1, waiting for transfers between devices, fetch_params(): lax.all_gather(wire_items[5], ('row', 'col'), axis=0, tiled=True)  89.6 us
    reduce_scatter x1, waiting for transfers between devices, on_device(): lax.psum_scatter(terms[1].astype(jnp.bfloat16), ('row', 'col'), scatter_d...  70.8 us
    psum x1, waiting for transfers between devices, on_device(): lax.psum(parted[0][0].astype(jnp.bfloat16), 'dp').astype(jnp.float32)  60.4 us
    reshape x12, local copies, waits for them, and re-layouts, unpack(): shard_item.reshape(row_count, col_count, shard_item.shape[1], shard_item....  57.4 us
    dot_general x6, matrix products, apply_weight(): jnp.einsum('trk,rckn->tcn', operand.reshape(token_count, row_count, rows_...  46.4 us
  transfers between devices with their start and end apart: 13, of which 7 were waited for; matrix products, arithmetic and copies ran while one was open for 17% of the time, Pallas kernels for 0%

commit v1 on v0

--- a/solution.py
+++ b/solution.py
@@ -315,7 +315,9 @@
         ).astype(jnp.float32),
     )
     summed = (
-        lax.psum(parted[0][0].astype(jnp.bfloat16), "dp").astype(jnp.float32),
+        jnp.sum(lax.all_gather(parted[0][0].astype(jnp.bfloat16), "dp"), axis=0).astype(
+            jnp.float32
+        ),
         lax.psum(parted[1][0].astype(jnp.bfloat16), "dp").astype(jnp.float32),
         lax.psum(parted[2][0].astype(jnp.bfloat16), "dp").astype(jnp.float32),
         lax.psum(parted[3][0].astype(jnp.bfloat16), "dp").astype(jnp.float32),

time: 1240 us -> 1280 us (1.032)
  waiting for transfers between devices: 630 us -> 665 us
    reduce_scatter x1, waiting for transfers between devices: 0.02 us -> 36.6 us  [on_device(): lax.psum_scatter(terms[2].astype(jnp.bfloat16), ('row', 'col'), scatter_d...]
  transfers between devices with their start and end apart: 13 -> 14, of which waited for: 7 -> 7; matrix products, arithmetic and copies ran while one was open for 17% -> 15% of each run, Pallas kernels for 0% -> 0%
where the time goes in v1:
time: 1280 us; the launch traced here: 1270 us
  waiting for transfers between devices  665 us (52%)
  blocking collectives  254 us (20%)
  matrix products  154 us (12%)
  local copies, waits for them, and re-layouts  124 us (10%)
  other arithmetic  54.8 us (4%)
  between operations  16.7 us (1%)
    reduce_scatter x1, waiting for transfers between devices, on_device(): lax.psum_scatter(terms[5].astype(jnp.bfloat16), ('row', 'col'), scatter_d...  150 us
    reduce_scatter x1, waiting for transfers between devices, on_device(): lax.psum_scatter(terms[4].astype(jnp.bfloat16), ('row', 'col'), scatter_d...  150 us
    all_gather x1, waiting for transfers between devices, fetch_params(): lax.all_gather(wire_items[4], ('row', 'col'), axis=0, tiled=True)  106 us
    all_gather x1, waiting for transfers between devices, fetch_params(): lax.all_gather(wire_items[5], ('row', 'col'), axis=0, tiled=True)  87.7 us
    reduce_scatter x1, waiting for transfers between devices, on_device(): lax.psum_scatter(terms[1].astype(jnp.bfloat16), ('row', 'col'), scatter_d...  71.4 us
    psum x1, waiting for transfers between devices, on_device(): lax.psum(parted[1][0].astype(jnp.bfloat16), 'dp').astype(jnp.float32)  62.1 us
    reshape x12, local copies, waits for them, and re-layouts, unpack(): shard_item.reshape(row_count, col_count, shard_item.shape[1], shard_item....  58.6 us
    dot_general x6, matrix products, apply_weight(): jnp.einsum('trk,rckn->tcn', operand.reshape(token_count, row_count, rows_...  46.8 us
  transfers between devices with their start and end apart: 14, of which 7 were waited for; matrix products, arithmetic and copies ran while one was open for 15% of the time, Pallas kernels for 0%

profile of v1, /device:TPU:0, one launch (start us, length us, event | category | flops | bytes accessed | tf_op | source)
XLA Modules:
  0.0 1269.4 jit_solution(3396390480290758911)
XLA Ops:
  19.2 22.3 %all-gather.16 = bf16[8,1,128]{2,1,0:T(2,128)(2,1)S(1)} all-gather(bf16[1,1,128]{2,1,0:T(2,128)(2,1)S(1)} %convert_bitcast_fusion.16), channel_id=5, replica_groups=mesh['dp'=4,'row'=2,'col'=4] {'row','col'}, dimensions={0}, use_global_device_ids=true | all-gather | bytes 2304 | tf_op jit(solution)/shard_map/all_gather | solution.py:92
  41.5 16.7 %all-gather.15 = bf16[8,1,128]{2,1,0:T(2,128)(2,1)S(1)} all-gather(bf16[1,1,128]{2,1,0:T(2,128)(2,1)S(1)} %convert_bitcast_fusion.17), channel_id=3, replica_groups=mesh['dp'=4,'row'=2,'col'=4] {'row','col'}, dimensions={0}, use_global_device_ids=true | all-gather | bytes 2304 | tf_op jit(solution)/shard_map/all_gather | solution.py:93
  58.3 18.8 %all-gather.17 = bf16[8,1,128]{2,1,0:T(2,128)(2,1)S(1)} all-gather(bf16[1,1,128]{2,1,0:T(2,128)(2,1)S(1)} %convert_bitcast_fusion.15), channel_id=8, replica_groups=mesh['dp'=4,'row'=2,'col'=4] {'row','col'}, dimensions={0}, use_global_device_ids=true | all-gather | bytes 2304 | tf_op jit(solution)/shard_map/all_gather | solution.py:94
  77.1 16.3 %all-gather.18 = bf16[8,1,128]{2,1,0:T(2,128)(2,1)S(1)} all-gather(bf16[1,1,128]{2,1,0:T(2,128)(2,1)S(1)} %convert_bitcast_fusion.14), channel_id=9, replica_groups=mesh['dp'=4,'row'=2,'col'=4] {'row','col'}, dimensions={0}, use_global_device_ids=true | all-gather | bytes 2304 | tf_op jit(solution)/shard_map/all_gather | solution.py:97
  93.4 18.8 %all-gather.19 = bf16[8,1,128]{2,1,0:T(2,128)(2,1)S(1)} all-gather(bf16[1,1,128]{2,1,0:T(2,128)(2,1)S(1)} %convert_bitcast_fusion.13), channel_id=10, replica_groups=mesh['dp'=4,'row'=2,'col'=4] {'row','col'}, dimensions={0}, use_global_device_ids=true | all-gather | bytes 2304 | tf_op jit(solution)/shard_map/all_gather | solution.py:98
  112.3 27.1 %all-gather.20 = bf16[8,1,512]{2,1,0:T(2,128)(2,1)S(1)} all-gather(bf16[1,1,512]{2,1,0:T(2,128)(2,1)S(1)} %reshape.564), channel_id=12, replica_groups=mesh['dp'=4,'row'=2,'col'=4] {'row','col'}, dimensions={0}, use_global_device_ids=true | all-gather | bytes 9216 | tf_op jit(solution)/shard_map/all_gather | solution.py:95
  139.4 16.5 %all-gather.21 = bf16[8,1,128]{2,1,0:T(2,128)(2,1)S(1)} all-gather(bf16[1,1,128]{2,1,0:T(2,128)(2,1)S(1)} %convert_bitcast_fusion.12), channel_id=14, replica_groups=mesh['dp'=4,'row'=2,'col'=4] {'row','col'}, dimensions={0}, use_global_device_ids=true | all-gather | bytes 2304 | tf_op jit(solution)/shard_map/all_gather | solution.py:96
  156.5 18.5 %all-gather.22 = bf16[8,1,128]{2,1,0:T(2,128)(2,1)S(1)} all-gather(bf16[1,1,128]{2,1,0:T(2,128)(2,1)S(1)} %convert_bitcast_fusion.11), channel_id=15, replica_groups=mesh['dp'=4,'row'=2,'col'=4] {'row','col'}, dimensions={0}, use_global_device_ids=true | all-gather | bytes 2304 | tf_op jit(solution)/shard_map/all_gather | solution.py:99
  175.6 16.3 %all-gather.23 = bf16[8,1,128]{2,1,0:T(2,128)(2,1)S(1)} all-gather(bf16[1,1,128]{2,1,0:T(2,128)(2,1)S(1)} %convert_bitcast_fusion.10), channel_id=16, replica_groups=mesh['dp'=4,'row'=2,'col'=4] {'row','col'}, dimensions={0}, use_global_device_ids=true | all-gather | bytes 2304 | tf_op jit(solution)/shard_map/all_gather | solution.py:100
  232.4 8.3 fusion
  251.7 87.7 %all-gather.44.cloned.1.call-done = bf16[16384,256]{1,0:T(8,128)(2,1)} async-done(((bf16[2048,256]{1,0:T(8,128)(2,1)}), bf16[16384,256]{1,0:T(8,128)(2,1)}) %all-gather.44.cloned.1.call-update) | async-done | bytes 8388624 | tf_op jit(solution)/shard_map/all_gather | solution.py:91
  339.4 11.7 copy.193
  358.3 105.7 %all-gather.42.cloned.1.call-done = bf16[4096,1024]{1,0:T(8,128)(2,1)} async-done(((bf16[512,1024]{1,0:T(8,128)(2,1)}), bf16[4096,1024]{1,0:T(8,128)(2,1)}) %all-gather.42.cloned.1.call-update) | async-done | bytes 8388624 | tf_op jit(solution)/shard_map/all_gather | solution.py:90
  464.0 11.5 copy.191
  483.1 25.7 %multiply_convert_fusion.1 = (bf16[512,4096]{1,0:T(8,128)(2,1)S(1)}, f32[512,4096]{1,0:T(8,128)}, f32[512,4096,1]{1,0,2:T(8,128)}) fusion(f32[4096]{0:T(1024)S(1)} %bitcast.410, bf16[4096,512,2]{1,0,2:T(8,128)(2,1)} %bitcast.353, bf16[64,2,8,512]{3,2,1,0:T(8,128)(2,1)S(1)} %bitcast.392), kind=kOutput, calls=%fused_computation.24 | convolution fusion | flops 4433379328 | bytes 30425088 | tf_op jit(solution)/shard_map/trk,rckn->tcn/dot_general | solution.py:26
  508.9 9.6 fusion.79
  524.6 14.8 %fusion.80 = (bf16[4096]{0:T(1024)(128)(2,1)}, bf16[512,4096]{1,0:T(8,128)(2,1)}) fusion(f32[512,4096]{1,0:T(8,128)} %get-tuple-element.60, bf16[4096,4,256]{2,0,1:T(8,128)(2,1)} %bitcast.351, bf16[64,4,8,256]{3,2,1,0:T(8,128)(2,1)S(1)} %bitcast.371, f32[4096]{0:T(1024)S(1)} %bitcast.411, f32[512,4096,1]{1,0,2:T(8,128)} %get-tuple-element.68), kind=kOutput, calls=%fused_computation.166 | convolution fusion | flops 4328517632 | bytes 30433280 | tf_op jit(solution)/shard_map/tcn,rckn->trk/dot_general | solution.py:38
  539.4 8.6 multiply_reduce_fusion.2
  553.8 14.9 %fusion.71 = (f32[16]{0:T(128)}, f32[16,512]{1,0:T(8,128)}, f32[16,512,512]{1,2,0:T(8,128)}) fusion(f32[16,512,512]{1,2,0:T(8,128)} %get-tuple-element.65, f32[16,512]{1,0:T(8,128)} %log_add_fusion, bf16[512,16,64]{0,2,1:T(8,128)(2,1)S(1)} %bitcast.346, bf16[512,16,64]{0,2,1:T(8,128)(2,1)} %bitcast.368), kind=kOutput, calls=%fused_computation.158 | convolution fusion | flops 553639936 | bytes 35717184 | tf_op jit(solution)/shard_map/sqhd,skhd->shqk/dot_general | solution.py:230
  570.6 8.0 multiply_convert_fusion
  596.7 8.7 bitcast_reduce_fusion
  622.0 9.0 convert_bitcast_fusion
  631.0 11.5 copy.225
  650.6 11.7 convert_bitcast_fusion.1
  662.3 11.5 copy.222
  680.7 38.5 %pmax.7 = f32[16]{0:T(128)S(1)} all-reduce(f32[16]{0:T(128)S(1)} %copy-done.52), channel_id=1, replica_groups=mesh['dp'=4,'row'=2,'col'=4] {'dp','row','col'}, use_global_device_ids=true, to_apply=%region_51.52 | all-reduce | flops 16 | bytes 128 | tf_op jit(solution)/shard_map/pmax | solution.py:209
  719.5 37.4 %all-reduce.9 = (bf16[8,128]{1,0:T(8,128)(2,1)S(1)}, bf16[8,128]{1,0:T(8,128)(2,1)S(1)}, bf16[8,128]{1,0:T(8,128)(2,1)S(1)}, bf16[8,512]{1,0:T(8,128)(2,1)S(1)},...) all-reduce(bf16[8,128]{1,0:T(8,128)(2,1)S(1)} %convert_element_type, ...), channel_id=23, replica_groups=mesh['dp'=4,'row'=2,'col'=4] {'row','col'}, use_global_device_ids=true, to_apply=%region_24.25.clone | all-reduce | flops 12288 | bytes 49152
  761.9 36.6 %reduce-scatter.11.cloned.1.call-done = bf16[1,512,256]{2,1,0:T(8,128)(2,1)} async-done(((bf16[8,512,256]{2,1,0:T(8,128)(2,1)}), bf16[1,512,256]{2,1,0:T(8,128)(2,1)}) %reduce-scatter.11.cloned.1.call-update) | async-done | bytes 262160 | tf_op jit(solution)/shard_map/reduce_scatter | solution.py:277
  798.5 71.4 %reduce-scatter.9.cloned.1.call-done = bf16[1,512,256]{2,1,0:T(8,128)(2,1)} async-done(((bf16[8,512,256]{2,1,0:T(8,128)(2,1)}), bf16[1,512,256]{2,1,0:T(8,128)(2,1)}) %reduce-scatter.9.cloned.1.call-update) | async-done | bytes 262160 | tf_op jit(solution)/shard_map/reduce_scatter | solution.py:274
  869.9 150.1 %reduce-scatter.17.cloned.1.call-done = bf16[1,2048,256]{2,1,0:T(8,128)(2,1)} async-done(((bf16[8,2048,256]{2,1,0:T(8,128)(2,1)}), bf16[1,2048,256]{2,1,0:T(8,128)(2,1)}) %reduce-scatter.17.cloned.1.call-update) | async-done | bytes 1048592 | tf_op jit(solution)/shard_map/reduce_scatter | solution.py:286
  1020.1 150.1 %reduce-scatter.15.cloned.1.call-done = bf16[1,512,1024]{2,1,0:T(8,128)(2,1)} async-done(((bf16[8,512,1024]{2,1,0:T(8,128)(2,1)}), bf16[1,512,1024]{2,1,0:T(8,128)(2,1)}) %reduce-scatter.15.cloned.1.call-update) | async-done | bytes 1048592 | tf_op jit(solution)/shard_map/reduce_scatter | solution.py:283
  1192.3 62.1 %all-reduce.14.cloned.1.call-done = (bf16[512,256]{1,0:T(8,128)(2,1)}, bf16[512,256]{1,0:T(8,128)(2,1)}, bf16[512,256]{1,0:T(8,128)(2,1)}, bf16[512,1024]{1,0:T(8,128)(2,1)}, bf16[2048,256]{1,0:T(8,128)(2,1)}) async-done(((bf16[512,256]{1,0:T(8,128)(2,1)}, bf16[512,256]{1,0:T(8,128)(2,1)}, bf16[512,256]{1,0:T(8,128)(2,1)}, bf16[512,1024]{1,0:T(8,128)(2,1)}, bf16[2048,256]{1,0:T(8,128)(2,1)}), ...) | async-done | bytes 2883600 | tf_op jit(solution)/shard_map/psum | solution.py:321
  (290 shorter events, 175.9 us)
Async XLA Ops:
  7.2 185.5 %all-gather.40.cloned.1.call-start = ((), (), s32[]{:S(2)}) async-start(), calls=%async_computation.16 | async-start | bytes 2359296 | tf_op jit(solution)/shard_map/all_gather | solution.py:89
  9.2 189.3 %all-gather.36.cloned.1.call-start = ((), (), s32[]{:S(2)}) async-start(), calls=%async_computation.14 | async-start | bytes 2359296 | tf_op jit(solution)/shard_map/all_gather | solution.py:86
  11.0 194.1 %all-gather.38.cloned.1.call-start = ((), (), s32[]{:S(2)}) async-start(), calls=%async_computation.15 | async-start | bytes 2359296 | tf_op jit(solution)/shard_map/all_gather | solution.py:87
  12.9 202.2 %all-gather.34.cloned.1.call-start = ((), (), s32[]{:S(2)}) async-start(), calls=%async_computation.13 | async-start | bytes 2359296 | tf_op jit(solution)/shard_map/all_gather | solution.py:88
  14.7 324.7 %all-gather.44.cloned.1.call-start = ((), (), s32[]{:S(2)}) async-start(), calls=%async_computation.18 | async-start | bytes 9437184 | tf_op jit(solution)/shard_map/all_gather | solution.py:91
  15.9 42.4 %copy-start.55 = (f32[128]{0:T(128)S(1)}, f32[128]{0:T(128)}, u32[]{:S(2)}) copy-start(f32[128]{0:T(128)} %param.31) | copy-start | bytes 1540
  15.9 61.2 %copy-start.56 = (f32[128]{0:T(128)S(1)}, f32[128]{0:T(128)}, u32[]{:S(2)}) copy-start(f32[128]{0:T(128)} %param.34) | copy-start | bytes 1540
  15.9 77.5 %copy-start.57 = (f32[128]{0:T(128)S(1)}, f32[128]{0:T(128)}, u32[]{:S(2)}) copy-start(f32[128]{0:T(128)} %param.35) | copy-start | bytes 1540
  15.9 96.3 %copy-start.51 = (f32[512]{0:T(512)S(1)}, f32[512]{0:T(512)}, u32[]{:S(2)}) copy-start(f32[512]{0:T(512)} %param.32) | copy-start | bytes 6148
  15.9 123.4 %copy-start.58 = (f32[128]{0:T(128)S(1)}, f32[128]{0:T(128)}, u32[]{:S(2)}) copy-start(f32[128]{0:T(128)} %param.33) | copy-start | bytes 1540
  15.9 140.6 %copy-start.59 = (f32[128]{0:T(128)S(1)}, f32[128]{0:T(128)}, u32[]{:S(2)}) copy-start(f32[128]{0:T(128)} %param.36) | copy-start | bytes 1540
  15.9 159.7 %copy-start.60 = (f32[128]{0:T(128)S(1)}, f32[128]{0:T(128)}, u32[]{:S(2)}) copy-start(f32[128]{0:T(128)} %param.37) | copy-start | bytes 1540
  15.9 176.6 %copy-start.42 = (s32[512]{0:T(512)S(1)}, s32[512]{0:T(512)}, u32[]{:S(2)}) copy-start(s32[512]{0:T(512)} %param.21) | copy-start | bytes 6148
  16.0 448.0 %all-gather.42.cloned.1.call-start = ((), (), s32[]{:S(2)}) async-start(), calls=%async_computation.17 | async-start | bytes 9437184 | tf_op jit(solution)/shard_map/all_gather | solution.py:90
  18.9 655.0 %reduce-scatter.7.cloned.1.call-start = ((), (), s32[]{:S(2)}) async-start(), calls=%async_computation.6 | async-start | bytes 2359296 | tf_op jit(solution)/shard_map/reduce_scatter | solution.py:271
  19.2 200.4 %copy-start.28 = (bf16[512,1024]{1,0:T(8,128)(2,1)}, bf16[512,1024]{1,0:T(8,128)(2,1)S(1)}, u32[]{:S(2)}) copy-start(bf16[512,1024]{1,0:T(8,128)(2,1)S(1)} %convert_element_type.490) | copy-start | bytes 3145732
  251.7 231.5 %copy-start.34 = (bf16[512,1024]{1,0:T(8,128)(2,1)}, bf16[512,1024]{1,0:T(8,128)(2,1)S(1)}, u32[]{:S(2)}) copy-start(bf16[512,1024]{1,0:T(8,128)(2,1)S(1)} %fusion.32) | copy-start | bytes 3145732
  589.7 172.2 %reduce-scatter.13.cloned.1.call-start = ((), (), s32[]{:S(2)}) async-start(), calls=%async_computation.10 | async-start | bytes 2359296 | tf_op jit(solution)/shard_map/reduce_scatter | solution.py:280
  596.6 201.9 %reduce-scatter.11.cloned.1.call-start = ((), (), s32[]{:S(2)}) async-start(), calls=%async_computation.9 | async-start | bytes 2359296 | tf_op jit(solution)/shard_map/reduce_scatter | solution.py:277
  610.1 259.8 %reduce-scatter.9.cloned.1.call-start = ((), (), s32[]{:S(2)}) async-start(), calls=%async_computation.8 | async-start | bytes 2359296 | tf_op jit(solution)/shard_map/reduce_scatter | solution.py:274
  621.1 398.9 %reduce-scatter.17.cloned.1.call-start = ((), (), s32[]{:S(2)}) async-start(), calls=%async_computation.12 | async-start | bytes 9437184 | tf_op jit(solution)/shard_map/reduce_scatter | solution.py:286
  642.5 527.6 %reduce-scatter.15.cloned.1.call-start = ((), (), s32[]{:S(2)}) async-start(), calls=%async_computation.11 | async-start | bytes 9437184 | tf_op jit(solution)/shard_map/reduce_scatter | solution.py:283
  673.9 516.1 %all-gather.32.cloned.1.call-start = ((), (), s32[]{:S(2)}) async-start(), calls=%async_computation.7 | async-start | bytes 1310720 | tf_op jit(solution)/shard_map/all_gather | solution.py:318
  674.7 579.7 %all-reduce.14.cloned.1.call-start = ((), (), s32[]{:S(2)}) async-start(), calls=%async_computation.19 | async-start | bytes 5767168 | tf_op jit(solution)/shard_map/psum | solution.py:321
  679.0 40.4 %copy-start.43 = (bf16[1024]{0:T(1024)(128)(2,1)S(1)}, bf16[1024]{0:T(1024)(128)(2,1)}, u32[]{:S(2)}) copy-start(bf16[1024]{0:T(1024)(128)(2,1)} %get-tuple-element.22) | copy-start | bytes 6148
  679.0 40.4 %copy-start.44 = (bf16[1024]{0:T(1024)(128)(2,1)S(1)}, bf16[1024]{0:T(1024)(128)(2,1)}, u32[]{:S(2)}) copy-start(bf16[1024]{0:T(1024)(128)(2,1)} %get-tuple-element.26) | copy-start | bytes 6148
  679.0 40.4 %copy-start.45 = (bf16[1024]{0:T(1024)(128)(2,1)S(1)}, bf16[1024]{0:T(1024)(128)(2,1)}, u32[]{:S(2)}) copy-start(bf16[1024]{0:T(1024)(128)(2,1)} %get-tuple-element.51) | copy-start | bytes 6148
  679.0 40.4 %copy-start.46 = (bf16[1024]{0:T(1024)(128)(2,1)S(1)}, bf16[1024]{0:T(1024)(128)(2,1)}, u32[]{:S(2)}) copy-start(bf16[1024]{0:T(1024)(128)(2,1)} %get-tuple-element.53) | copy-start | bytes 6148
  679.0 40.4 %copy-start.49 = (bf16[1024]{0:T(1024)(128)(2,1)S(1)}, bf16[1024]{0:T(1024)(128)(2,1)}, u32[]{:S(2)}) copy-start(bf16[1024]{0:T(1024)(128)(2,1)} %get-tuple-element.24) | copy-start | bytes 6148
  679.1 40.4 %copy-start.50 = (bf16[1024]{0:T(1024)(128)(2,1)S(1)}, bf16[1024]{0:T(1024)(128)(2,1)}, u32[]{:S(2)}) copy-start(bf16[1024]{0:T(1024)(128)(2,1)} %get-tuple-element.27) | copy-start | bytes 6148
  680.5 501.6 %copy-start.21 = (bf16[16,64,512]{2,1,0:T(8,128)(2,1)S(1)}, bf16[16,64,512]{2,1,0:T(8,128)(2,1)}, u32[]{:S(2)}) copy-start(bf16[16,64,512]{2,1,0:T(8,128)(2,1)} %copy-done.20) | copy-start | bytes 3145732
  719.2 465.9 %copy-start.64 = (f32[16]{0:T(128)}, f32[16]{0:T(128)S(1)}, u32[]{:S(2)}) copy-start(f32[16]{0:T(128)S(1)} %pmax.7) | copy-start | bytes 196
  (53 other events, 420.5 us)
Sparse Core Ops, SparseCore 0:
  10.7 51.8 all-gather.39
  65.3 47.7 all-gather.35
  115.8 47.7 all-gather.37
  166.1 47.6 all-gather.33
  216.3 122.9 all-gather.43
  341.4 122.6 all-gather.41
  589.8 66.4 reduce-scatter.6
  659.9 67.7 reduce-scatter.12
  731.1 67.3 reduce-scatter.10
  802.5 67.3 reduce-scatter.8
  873.5 146.4 reduce-scatter.16
  1023.5 146.5 reduce-scatter.14
  1171.7 15.7 all-gather.31
  1190.1 64.2 all-reduce.13
